TPU v7x, 256 devices: a whole 4x4x8 slice. The times are simulated.
256 devices in a mesh: context: 32 (over x, z), mirror: 2 (over core), tensor: 4 (over y).
Axes of the slice: x: 4, y: 4, z: 8, core: 2. Of those that a mesh axis runs over, the one named last changes fastest.
Arguments:
- hyena_q: bfloat16 [8192, 8192], P(('context', 'mirror'), 'tensor'), may hold values from -57 to 57
- hyena_k: bfloat16 [8192, 8192], P(('context', 'mirror'), 'tensor'), may hold values from -6 to 6
- hyena_v: bfloat16 [8192, 8192], P(('context', 'mirror'), 'tensor'), may hold values from -6 to 6
- filters: bfloat16 [512, 128], P('tensor'), may hold values from -0.5 to 0.5
- norm_gain: float32 [8192], P('tensor'), may hold values from 0.1 to 1.9
- attn_q: bfloat16 [8192, 8192], P(('context', 'mirror'), 'tensor'), may hold values from -35 to 35
- attn_k: bfloat16 [8192, 8192], P(('context', 'mirror'), 'tensor'), may hold values from -5 to 5
- out_grad: bfloat16 [8192, 8192], P(('context', 'mirror'), 'tensor'), may hold values from -20 to 20
- doc_lengths: int32 [4], replicated, may hold values from 1 to 4096, 8192 in all
Outputs:
- attn_out: bfloat16 [8192, 8192], P(('context', 'mirror'), 'tensor')
- grad_attn_q: bfloat16 [8192, 8192], P(('context', 'mirror'), 'tensor')
- grad_attn_k: bfloat16 [8192, 8192], P(('context', 'mirror'), 'tensor')
- grad_hyena_q: bfloat16 [8192, 8192], P(('context', 'mirror'), 'tensor')
- grad_hyena_k: bfloat16 [8192, 8192], P(('context', 'mirror'), 'tensor')
- grad_hyena_v: bfloat16 [8192, 8192], P(('context', 'mirror'), 'tensor')
- grad_filters: float32 [512, 128], P('tensor')
All inputs are finite; a program needn't handle non-finite values.
Results may differ from a plain program's by a relative error of at most 0.0064.
Values may be sent and summed in bfloat16 or wider, within the bound.
No kernel may reach another device: no remote copies, remote signals or barrier semaphores. Data moves between devices by JAX's collectives and lax.ppermute only.
A program may use at most 128 MiB of HBM per device.

v0:
```python
import jax
import jax.numpy as jnp
from jax import lax
from jax.sharding import PartitionSpec as P

HEAD = 128
D = 8192
REACH = 2


def passed_along(block, axis, distance):
    devices = range(lax.axis_size(axis))
    route = [(i - distance, i) for i in devices if i - distance in devices]
    return lax.ppermute(block, axis, route)


def doc_index(doc_lengths, positions):
    doc_ends = jnp.cumsum(doc_lengths, dtype=jnp.int32)
    return jnp.sum(
        (positions[:, None] >= doc_ends[None, :]).astype(jnp.int32), axis=1, dtype=jnp.int32
    )


def banded(band_table, row_count, col_count):
    repeated = jnp.tile(band_table, (1, row_count + 1))[:, : row_count * col_count]
    return repeated.reshape(band_table.shape[0], row_count, col_count)


def attend(queries, key_heads, allowed, score_scale):
    scores = (
        jnp.einsum("thd,uhd->htu", queries, key_heads, preferred_element_type=jnp.float32)
        * score_scale
    )
    row_top = jnp.max(jnp.where(allowed[None], scores, -1e30), axis=2, keepdims=True)
    row_total = jnp.sum(
        jnp.exp(jnp.where(allowed[None], scores - row_top, -1e30)), axis=2, keepdims=True
    )
    row_lse = row_top + jnp.log(row_total)
    return (jnp.where(allowed[None], jnp.exp(scores - row_lse), 0.0), row_lse)


def body(hyena_q, hyena_k, hyena_v, filters, norm_gain, attn_q, attn_k, out_grad, doc_lengths):
    tok_rows, channels = hyena_q.shape
    groups, tap_count = filters.shape
    group_width = channels // groups
    heads_dev = channels // HEAD
    pad_rows = tok_rows + tap_count
    offset = lax.axis_index(("context", "mirror")) * tok_rows
    score_scale = HEAD ** (-0.5)
    window_span = REACH * tok_rows
    own_pos = offset + jnp.arange(tok_rows, dtype=jnp.int32)
    own_doc = doc_index(doc_lengths, own_pos)
    kv_product = (hyena_k.astype(jnp.float32) * hyena_v.astype(jnp.float32)).astype(jnp.bfloat16)
    left_rim = passed_along(kv_product[tok_rows - (tap_count - 1) :], ("context", "mirror"), 1)
    wide_pad = jnp.concatenate(
        [left_rim, kv_product, jnp.zeros((1, channels), jnp.bfloat16)], axis=0
    )
    wide_pos = offset - (tap_count - 1) + jnp.arange(pad_rows, dtype=jnp.int32)
    fwd_mask = own_doc[:, None] == doc_index(doc_lengths, wide_pos)[None, :]
    zeros_tail = jnp.zeros((groups, pad_rows + 1 - tap_count), jnp.bfloat16)
    fwd_table = jnp.concatenate([filters[:, ::-1], zeros_tail], axis=1)
    fwd_band = banded(fwd_table, tok_rows, pad_rows) * fwd_mask[None].astype(jnp.bfloat16)
    wide_groups = wide_pad.reshape(pad_rows, groups, group_width)
    signal = jnp.einsum(
        "gtu,ugc->tgc", fwd_band, wide_groups, preferred_element_type=jnp.float32
    ).reshape(tok_rows, channels)
    hyena_mix = hyena_q.astype(jnp.float32) * signal
    square_sum = lax.psum(jnp.sum(hyena_mix * hyena_mix, axis=1), "tensor")
    inv_rms = lax.rsqrt(square_sum / D + 1e-06)
    values = (hyena_mix * inv_rms[:, None] * norm_gain[None, :]).astype(jnp.bfloat16)
    earlier = []
    for distance in range(1, REACH + 1):
        earlier.append(passed_along((attn_k, values), ("context", "mirror"), distance))
    key_win = jnp.concatenate([piece[0] for piece in earlier[::-1]] + [attn_k], axis=0)
    value_win = jnp.concatenate([piece[1] for piece in earlier[::-1]] + [values], axis=0)
    window = (REACH + 1) * tok_rows
    key_pos = offset - REACH * tok_rows + jnp.arange(window, dtype=jnp.int32)
    key_doc = doc_index(doc_lengths, key_pos)
    allowed = (
        (key_pos[None, :] >= 0)
        & (key_pos[None, :] <= own_pos[:, None])
        & (own_pos[:, None] - key_pos[None, :] <= window_span)
        & (key_doc[None, :] == own_doc[:, None])
    )
    queries = attn_q.reshape(tok_rows, heads_dev, HEAD)
    grad_heads = out_grad.reshape(tok_rows, heads_dev, HEAD)
    key_heads = key_win.reshape(window, heads_dev, HEAD)
    value_heads = value_win.reshape(window, heads_dev, HEAD)
    attn_prob, row_lse = attend(queries, key_heads, allowed, score_scale)
    prob_half = attn_prob.astype(jnp.bfloat16)
    attn_out = (
        jnp.einsum("htu,uhd->thd", prob_half, value_heads, preferred_element_type=jnp.float32)
        .astype(jnp.bfloat16)
        .reshape(tok_rows, channels)
    )
    grad_prob = jnp.einsum(
        "thd,uhd->htu", grad_heads, value_heads, preferred_element_type=jnp.float32
    )
    row_delta = jnp.sum(attn_prob * grad_prob, axis=2, keepdims=True)
    grad_score = (attn_prob * (grad_prob - row_delta) * score_scale).astype(jnp.bfloat16)
    grad_attn_q = (
        jnp.einsum("htu,uhd->thd", grad_score, key_heads, preferred_element_type=jnp.float32)
        .astype(jnp.bfloat16)
        .reshape(tok_rows, channels)
    )
    own_start = REACH * tok_rows
    key_part = jnp.einsum("htu,thd->uhd", grad_score, queries, preferred_element_type=jnp.float32)
    value_part = jnp.einsum(
        "htu,thd->uhd", prob_half, grad_heads, preferred_element_type=jnp.float32
    )
    grad_keys = key_part[own_start:]
    grad_vals = value_part[own_start:]
    for distance in range(1, REACH + 1):
        low_row = (REACH - distance) * tok_rows
        returned = passed_along(
            (key_part[low_row : low_row + tok_rows], value_part[low_row : low_row + tok_rows]),
            ("context", "mirror"),
            -distance,
        )
        grad_keys = grad_keys + returned[0]
        grad_vals = grad_vals + returned[1]
    grad_attn_k = grad_keys.astype(jnp.bfloat16).reshape(tok_rows, channels)
    grad_values = grad_vals.reshape(tok_rows, channels)
    inner_sum = lax.psum(jnp.sum(norm_gain[None, :] * grad_values * hyena_mix, axis=1), "tensor")
    grad_mix = inv_rms[:, None] * (
        norm_gain[None, :] * grad_values - hyena_mix * (inner_sum * inv_rms * inv_rms / D)[:, None]
    )
    grad_hyena_q = (grad_mix * signal).astype(jnp.bfloat16)
    grad_signal = (grad_mix * hyena_q.astype(jnp.float32)).astype(jnp.bfloat16)
    right_rim = passed_along(grad_signal[: tap_count - 1], ("context", "mirror"), -1)
    back_pad = jnp.concatenate(
        [grad_signal, right_rim, jnp.zeros((1, channels), jnp.bfloat16)], axis=0
    )
    back_pos = offset + jnp.arange(pad_rows, dtype=jnp.int32)
    back_mask = own_doc[:, None] == doc_index(doc_lengths, back_pos)[None, :]
    back_table = jnp.concatenate([filters, zeros_tail], axis=1)
    back_band = banded(back_table, tok_rows, pad_rows) * back_mask[None].astype(jnp.bfloat16)
    grad_kv = jnp.einsum(
        "gtu,ugc->tgc",
        back_band,
        back_pad.reshape(pad_rows, groups, group_width),
        preferred_element_type=jnp.float32,
    ).reshape(tok_rows, channels)
    grad_hyena_k = (grad_kv * hyena_v.astype(jnp.float32)).astype(jnp.bfloat16)
    grad_hyena_v = (grad_kv * hyena_k.astype(jnp.float32)).astype(jnp.bfloat16)
    block_count = 4
    block_size = groups // block_count
    mask_float = fwd_mask.astype(jnp.float32)

    def filter_block(pieces):
        grad_block, wide_block = pieces
        correlation = (
            jnp.einsum("tgc,ugc->gtu", grad_block, wide_block, preferred_element_type=jnp.float32)
            * mask_float[None]
        )
        flattened = jnp.pad(
            correlation.reshape(block_size, tok_rows * pad_rows), ((0, 0), (0, tok_rows))
        )
        diagonal = flattened.reshape(block_size, tok_rows, pad_rows + 1)[:, :, :tap_count]
        return jnp.sum(diagonal, axis=1)[:, ::-1]

    grad_blocks = grad_signal.reshape(tok_rows, block_count, block_size, group_width).transpose(
        1, 0, 2, 3
    )
    wide_blocks = wide_groups.reshape(pad_rows, block_count, block_size, group_width).transpose(
        1, 0, 2, 3
    )
    local_filters = lax.map(filter_block, (grad_blocks, wide_blocks)).reshape(groups, tap_count)
    grad_filters = lax.psum(local_filters, ("context", "mirror"))
    return (
        attn_out,
        grad_attn_q,
        grad_attn_k,
        grad_hyena_q,
        grad_hyena_k,
        grad_hyena_v,
        grad_filters,
    )


def solution(mesh):
    return jax.shard_map(
        body,
        mesh=mesh,
        in_specs=(
            P(("context", "mirror"), "tensor"),
            P(("context", "mirror"), "tensor"),
            P(("context", "mirror"), "tensor"),
            P("tensor", None),
            P("tensor"),
            P(("context", "mirror"), "tensor"),
            P(("context", "mirror"), "tensor"),
            P(("context", "mirror"), "tensor"),
            P(),
        ),
        out_specs=(
            P(("context", "mirror"), "tensor"),
            P(("context", "mirror"), "tensor"),
            P(("context", "mirror"), "tensor"),
            P(("context", "mirror"), "tensor"),
            P(("context", "mirror"), "tensor"),
            P(("context", "mirror"), "tensor"),
            P("tensor", None),
        ),
        check_vma=False,
    )
```

profile of v0, /device:TPU:1, one launch (start us, length us, event | category | flops | bytes accessed | tf_op | source)
XLA Modules:
  0.0 418.3 jit_solution(6076285192775258305)
XLA Ops:
  8.6 5.1 %collective-permute-start.4 = (bf16[128,2048]{0,1:T(8,128)(2,1)S(1)}, bf16[128,2048]{0,1:T(8,128)(2,1)}, u32[]{:S(2)}, u32[]{:S(2)}) collective-permute-start(bf16[128,2048]{0,1:T(8,128)(2,1)S(1)} %copy.70), channel_id=1, source_target_pairs={{0,4},{4,8},{8,12},{12,16},{16,20},{20,24},{24,28},{28,32},{32,36}... | collective-permute-start | bytes 1572872 | tf_op jit(solution)/shard_map/ppermute | solution.py:14
  13.7 4.4 %collective-permute-start.3 = (bf16[128,2048]{0,1:T(8,128)(2,1)S(1)}, bf16[128,2048]{0,1:T(8,128)(2,1)}, u32[]{:S(2)}, u32[]{:S(2)}) collective-permute-start(bf16[128,2048]{0,1:T(8,128)(2,1)S(1)} %copy.70), channel_id=1, source_target_pairs={{0,8},{4,12},{8,16},{12,20},{16,24},{20,28},{24,32},{28,36},{32,40... | collective-permute-start | bytes 1572872 | tf_op jit(solution)/shard_map/ppermute | solution.py:14
  19.4 1.5 copy.66
  22.9 1.9 collective-permute-start
  28.5 4.5 %tile.8 = bf16[128,129,257]{0,2,1:T(8,128)(2,1)} broadcast(bf16[128,257]{0,1:T(8,128)(2,1)S(1)} %concatenate.19.clone), dimensions={0,2} | broadcast | bytes 8552960 | tf_op jit(solution)/shard_map/tile | solution.py:25
  33.0 13.2 %tile.9 = bf16[128,33153]{0,1:T(8,128)(2,1)} reshape(bf16[128,129,257]{0,2,1:T(8,128)(2,1)} %tile.8) | data formatting | bytes 16974336 | tf_op jit(solution)/shard_map/tile | solution.py:25
  46.3 7.1 %slice.49 = bf16[128,32768]{0,1:T(8,128)(2,1)} slice(bf16[128,33153]{0,1:T(8,128)(2,1)} %tile.9), slice={[0:128], [0:32768]} | slice | bytes 16777216 | tf_op jit(solution)/shard_map/slice | solution.py:25
  53.3 12.5 %copy.69 = bf16[128,128,256]{2,1,0:T(8,128)(2,1)} copy(bf16[128,128,256]{0,2,1:T(8,128)(2,1)} %bitcast.165) | data formatting | bytes 16777216 | tf_op jit(solution)/shard_map/reshape | solution.py:26
  65.8 4.5 %tile.20 = bf16[128,129,257]{0,2,1:T(8,128)(2,1)} broadcast(bf16[128,257]{0,1:T(8,128)(2,1)S(1)} %concatenate.23.clone), dimensions={0,2} | broadcast | bytes 8552960 | tf_op jit(solution)/shard_map/tile | solution.py:25
  70.3 13.2 %tile.21 = bf16[128,33153]{0,1:T(8,128)(2,1)} reshape(bf16[128,129,257]{0,2,1:T(8,128)(2,1)} %tile.20) | data formatting | bytes 16974336 | tf_op jit(solution)/shard_map/tile | solution.py:25
  83.5 7.1 %slice.57 = bf16[128,32768]{0,1:T(8,128)(2,1)} slice(bf16[128,33153]{0,1:T(8,128)(2,1)} %tile.21), slice={[0:128], [0:32768]} | slice | bytes 16777216 | tf_op jit(solution)/shard_map/slice | solution.py:25
  90.6 12.6 %copy.84 = bf16[128,128,256]{2,1,0:T(8,128)(2,1)} copy(bf16[128,128,256]{0,2,1:T(8,128)(2,1)} %bitcast.166) | data formatting | bytes 16777216 | tf_op jit(solution)/shard_map/reshape | solution.py:26
  103.7 1.4 pad_maximum_fusion.1
  107.7 1.6 collective-permute-start.8
  109.3 3.4 collective-permute-start.7
  112.7 1.5 maximum_maximum_fusion
  114.2 2.3 fusion.10
  116.6 16.7 %collective-permute-done.8 = f32[128,16,128]{0,2,1:T(8,128)S(1)} collective-permute-done((f32[128,16,128]{0,2,1:T(8,128)S(1)}, f32[128,16,128]{0,2,1:T(8,128)S(1)}, u32[]{:S(2)}, u32[]{:S(2)}) %collective-permute-start.8) | collective-permute-done | bytes 1048608 | tf_op jit(solution)/shard_map/ppermute | solution.py:14
  133.3 12.7 %collective-permute-done.7 = f32[128,16,128]{0,2,1:T(8,128)S(1)} collective-permute-done((f32[128,16,128]{0,2,1:T(8,128)S(1)}, f32[128,16,128]{0,2,1:T(8,128)S(1)}, u32[]{:S(2)}, u32[]{:S(2)}) %collective-permute-start.7) | collective-permute-done | bytes 1048608 | tf_op jit(solution)/shard_map/ppermute | solution.py:14
  147.2 8.7 %all-reduce.3 = (f32[128]{0:T(128)S(1)}, f32[128]{0:T(128)S(1)}) all-reduce(f32[128]{0:T(128)S(1)} %get-tuple-element.111, f32[128]{0:T(128)S(1)} %get-tuple-element.110), channel_id=1, replica_groups=mesh['context'=32,'mirror'=2,'tensor'=4] {'tensor'}, use_global_device_ids=true, to_apply=%region_4.5 | all-reduce | flops 256 | bytes 2048 | tf_op jit(solution)/shard_map/psum | solution.py:68
  155.9 3.4 fusion.45
  159.2 3.8 collective-permute-start.2
  163.0 5.2 %collective-permute-start.1 = (bf16[128,2048]{0,1:T(8,128)(2,1)}, bf16[128,2048]{0,1:T(8,128)(2,1)}, u32[]{:S(2)}, u32[]{:S(2)}) collective-permute-start(bf16[128,2048]{0,1:T(8,128)(2,1)} %get-tuple-element.134), channel_id=1, source_target_pairs={{0,8},{4,12},{8,16},{12,20},{16,24},{20,28},{24,32},{28,36},{32,40... | collective-permute-start | bytes 1572872 | tf_op jit(solution)/shard_map/ppermute | solution.py:14
  168.2 1.9 collective-permute-start.9
  170.1 67.7 %while.13 = (s32[]{:T(128)}, f32[4,32,128]{2,1,0:T(8,128)}, bf16[4,128,32,16]{1,3,2,0:T(8,128)(2,1)}, bf16[4,256,32,16]{1,3,2,0:T(8,128)(2,1)}, s32[256]{0:T(256...) while((s32[]{:T(128)}, f32[4,32,128]{2,1,0:T(8,128)}, bf16[4,128,32,16]{1,3,2,0:T(8,128)(2,1)}, ...), condition=%wide.region_14.15_spmd.clone, body=%wide.region_12.14_spmd.clone.sunk | while | flops 35188736 | bytes 32246372 | solution.py:168
  170.2 1.8 convolution_multiply_fusion.2
  172.0 2.4 copy.103
  174.5 2.2 pad.33
  176.7 8.0 %reshape.319 = f32[32,128,257]{2,1,0:T(8,128)} reshape(f32[32,32896]{1,0:T(8,128)} %pad.33) | data formatting | bytes 8421376 | tf_op jit(solution)/shard_map/while/body/eval_jaxpr/reshape | solution.py:159
  184.7 1.7 slice_reduce_fusion.2
  187.2 1.8 convolution_multiply_fusion.2
  188.9 2.4 copy.103
  191.4 2.2 pad.33
  193.6 8.0 %reshape.319 = f32[32,128,257]{2,1,0:T(8,128)} reshape(f32[32,32896]{1,0:T(8,128)} %pad.33) | data formatting | bytes 8421376 | tf_op jit(solution)/shard_map/while/body/eval_jaxpr/reshape | solution.py:159
  201.6 1.7 slice_reduce_fusion.2
  204.1 1.8 convolution_multiply_fusion.2
  205.9 2.4 copy.103
  208.3 2.2 pad.33
  210.6 8.0 %reshape.319 = f32[32,128,257]{2,1,0:T(8,128)} reshape(f32[32,32896]{1,0:T(8,128)} %pad.33) | data formatting | bytes 8421376 | tf_op jit(solution)/shard_map/while/body/eval_jaxpr/reshape | solution.py:159
  218.5 1.7 slice_reduce_fusion.2
  221.0 1.8 convolution_multiply_fusion.2
  222.8 2.4 copy.103
  225.2 2.2 pad.33
  227.5 8.0 %reshape.319 = f32[32,128,257]{2,1,0:T(8,128)} reshape(f32[32,32896]{1,0:T(8,128)} %pad.33) | data formatting | bytes 8421376 | tf_op jit(solution)/shard_map/while/body/eval_jaxpr/reshape | solution.py:159
  235.4 1.7 slice_reduce_fusion.2
  237.8 2.0 copy.88
  239.9 1.4 maximum_maximum_fusion.1
  241.4 6.7 %fusion.8 = f32[128,16,128]{2,1,0:T(8,128)} fusion(bf16[256,128,16]{0,2,1:T(8,128)(2,1)S(1)} %bitcast.175, bf16[128,128,256]{2,1,0:T(8,128)(2,1)} %copy.84, bf16[128,256]{1,0:T(8,128)(2,1)S(1)} %get-tuple-element.137), kind=kOutput, calls=%fused_computation.11 | convolution fusion | flops 138412032 | bytes 10551296 | tf_op jit(solution)/shard_map/gtu,ugc->tgc/dot_general | solution.py:138
  248.1 1.6 pad_maximum_fusion
  250.9 2.3 fusion.72
  253.2 6.6 %convolution_bitcast_fusion.1 = f32[384,16,128]{0,2,1:T(8,128)} fusion(bf16[128,16,128]{0,2,1:T(8,128)(2,1)} %bitcast.177, f32[16,384,128]{2,1,0:T(8,128)} %fusion.72, f32[16,384,128]{2,1,0:T(8,128)S(1)} %get-tuple-element.142, f32[16,128]{1,0:T(8,128)S(1)} %log_add_fusion, pred[128,384]{0,1:T(8,128)(4,1)S(1)} %fusion.54), kind=kOutput, calls=%fused_computation.32 | convolution fusion | flops 209979776 | bytes 10018816 | tf_op jit(solution)/shard_map/htu,thd->uhd/dot_general | solution.py:107
  259.8 3.4 fusion.70
  264.5 2.1 collective-permute-start.5
  267.8 2.0 copy.89
  269.9 2.0 copy.90
  271.9 3.0 convolution_convert_fusion
  274.9 2.0 copy.85
  276.9 6.2 %fusion.44 = bf16[16,128,128]{2,1,0:T(8,128)(2,1)} fusion(bf16[384,16,128]{0,2,1:T(8,128)(2,1)} %bitcast.172, f32[16,384,128]{2,1,0:T(8,128)} %fusion.72, f32[16,384,128]{2,1,0:T(8,128)S(1)} %get-tuple-element.142, f32[16,128]{1,0:T(8,128)S(1)} %log_add_fusion, pred[128,384]{0,1:T(8,128)(4,1)S(1)} %fusion.54), kind=kOutput, calls=%fused_computation.54 | convolution fusion | flops 210241920 | bytes 8445952 | tf_op jit(solution)/shard_map/htu,uhd->thd/dot_general | solution.py:102
  283.1 2.0 copy.86
  285.2 5.1 %collective-permute-done.6 = f32[128,16,128]{0,2,1:T(8,128)} collective-permute-done((f32[128,16,128]{0,2,1:T(8,128)}, f32[128,16,128]{0,2,1:T(8,128)}, u32[]{:S(2)}, u32[]{:S(2)}) %collective-permute-start.6) | collective-permute-done | bytes 1048608 | tf_op jit(solution)/shard_map/ppermute | solution.py:14
  290.3 11.6 %collective-permute-done.5 = f32[128,16,128]{0,2,1:T(8,128)} collective-permute-done((f32[128,16,128]{0,2,1:T(8,128)}, f32[128,16,128]{0,2,1:T(8,128)}, u32[]{:S(2)}, u32[]{:S(2)}) %collective-permute-start.5) | collective-permute-done | bytes 1048608 | tf_op jit(solution)/shard_map/ppermute | solution.py:14
  301.8 2.0 fusion.51
  304.9 105.0 %all-reduce.6.cloned.1.call-done = f32[128,128]{1,0:T(8,128)} async-done(((f32[128,128]{1,0:T(8,128)}), f32[128,128]{1,0:T(8,128)}) %all-reduce.6.cloned.1.call-update) | async-done | bytes 65552 | tf_op jit(solution)/shard_map/psum | solution.py:169
  410.0 1.5 copy.114
  (104 shorter events, 20.3 us)
Async XLA Ops:
  7.2 17.6 %copy-start.19 = (bf16[128,128]{1,0:T(8,128)(2,1)S(1)}, bf16[128,128]{1,0:T(8,128)(2,1)}, u32[]{:S(2)}) copy-start(bf16[128,128]{1,0:T(8,128)(2,1)} %param.14) | copy-start | bytes 98308
  7.2 17.9 %copy-start.16 = (bf16[128,2048]{1,0:T(8,128)(2,1)S(1)}, bf16[128,2048]{1,0:T(8,128)(2,1)}, u32[]{:S(2)}) copy-start(bf16[128,2048]{1,0:T(8,128)(2,1)} %param.11) | copy-start | bytes 1572868
  7.2 402.8 %all-reduce.6.cloned.1.call-start = ((), (), s32[]{:S(2)}) async-start(), calls=%async_computation | async-start | bytes 131072 | tf_op jit(solution)/shard_map/psum | solution.py:169
  8.6 17.4 %copy-start.17 = (bf16[128,2048]{1,0:T(8,128)(2,1)S(1)}, bf16[128,2048]{1,0:T(8,128)(2,1)}, u32[]{:S(2)}) copy-start(bf16[128,2048]{1,0:T(8,128)(2,1)} %param.18) | copy-start | bytes 1572868
  8.6 95.0 %collective-permute-start.4 = (bf16[128,2048]{0,1:T(8,128)(2,1)S(1)}, bf16[128,2048]{0,1:T(8,128)(2,1)}, u32[]{:S(2)}, u32[]{:S(2)}) collective-permute-start(bf16[128,2048]{0,1:T(8,128)(2,1)S(1)} %copy.70), channel_id=1, source_target_pairs={{0,4},{4,8},{8,12},{12,16},{16,20},{20,24},{24,28},{28,32},{32,36}... | collective-permute-start | bytes 1572872 | tf_op jit(solution)/shard_map/ppermute | solution.py:14
  13.7 90.0 %collective-permute-start.3 = (bf16[128,2048]{0,1:T(8,128)(2,1)S(1)}, bf16[128,2048]{0,1:T(8,128)(2,1)}, u32[]{:S(2)}, u32[]{:S(2)}) collective-permute-start(bf16[128,2048]{0,1:T(8,128)(2,1)S(1)} %copy.70), channel_id=1, source_target_pairs={{0,8},{4,12},{8,16},{12,20},{16,24},{20,28},{24,32},{28,36},{32,40... | collective-permute-start | bytes 1572872 | tf_op jit(solution)/shard_map/ppermute | solution.py:14
  19.3 9.1 %copy-start.8 = (bf16[128,2048]{0,1:T(8,128)(2,1)}, bf16[128,2048]{0,1:T(8,128)(2,1)S(1)}, u32[]{:S(2)}) copy-start(bf16[128,2048]{0,1:T(8,128)(2,1)S(1)} %copy.67) | copy-start | bytes 1572868
  19.4 7.7 %copy-start.21 = (s32[4]{0:T(128)S(1)}, s32[4]{0:T(128)}, u32[]{:S(2)}) copy-start(s32[4]{0:T(128)} %param.19) | copy-start | bytes 52
  19.4 8.0 %copy-start.18 = (bf16[128,2048]{1,0:T(8,128)(2,1)S(1)}, bf16[128,2048]{1,0:T(8,128)(2,1)}, u32[]{:S(2)}) copy-start(bf16[128,2048]{1,0:T(8,128)(2,1)} %param.16) | copy-start | bytes 1572868
  20.9 12.1 %copy-start.10 = (bf16[128,2048]{0,1:T(8,128)(2,1)}, bf16[128,2048]{0,1:T(8,128)(2,1)S(1)}, u32[]{:S(2)}) copy-start(bf16[128,2048]{0,1:T(8,128)(2,1)S(1)} %copy.66) | copy-start | bytes 1572868
  21.1 0.8 copy-start.6
  22.9 89.8 %collective-permute-start = (bf16[127,2048]{0,1:T(8,128)(2,1)}, bf16[127,2048]{0,1:T(8,128)(2,1)}, u32[]{:S(2)}, u32[]{:S(2)}) collective-permute-start(bf16[127,2048]{0,1:T(8,128)(2,1)} %slice.48), channel_id=1, source_target_pairs={{0,4},{4,8},{8,12},{12,16},{16,20},{20,24},{24,28},{28,32},{32,36}... | collective-permute-start | bytes 1560584 | tf_op jit(solution)/shard_map/ppermute | solution.py:14
  103.1 1.9 copy-start.15
  105.1 1.5 copy-start.4
  105.1 1.5 copy-start.12
  105.9 8.3 %slice-start = ((s8[8388608]{0:T(1024)(128)(4,1)}), s8[4194304]{0:T(1024)(128)(4,1)S(1)}, s32[]{:S(2)}) async-start(s8[8388608]{0:T(1024)(128)(4,1)} %bitcast.163), calls=%async_computation.1 | async-start | bytes 8388608
  106.6 7.6 %slice-start.1 = ((s8[8388608]{0:T(1024)(128)(4,1)}), s8[4194304]{0:T(1024)(128)(4,1)S(1)}, s32[]{:S(2)}) async-start(s8[8388608]{0:T(1024)(128)(4,1)} %bitcast.163), calls=%async_computation.2 | async-start | bytes 8388608
  107.4 5.2 %copy-start.7 = (bf16[128,2048]{0,1:T(8,128)(2,1)S(1)}, bf16[128,2048]{0,1:T(8,128)(2,1)}, u32[]{:S(2)}) copy-start(bf16[128,2048]{0,1:T(8,128)(2,1)} %copy-done.6) | copy-start | bytes 1572868
  107.7 25.6 %collective-permute-start.8 = (f32[128,16,128]{0,2,1:T(8,128)S(1)}, f32[128,16,128]{0,2,1:T(8,128)S(1)}, u32[]{:S(2)}, u32[]{:S(2)}) collective-permute-start(f32[128,16,128]{0,2,1:T(8,128)S(1)} %get-tuple-element.131), channel_id=1, source_target_pairs={{8,0},{12,4},{16,8},{20,12},{24,16},{28,20},{32,24},{36,28},{40,32... | collective-permute-start | bytes 3145736 | tf_op jit(solution)/shard_map/ppermute | solution.py:14
  109.3 36.7 %collective-permute-start.7 = (f32[128,16,128]{0,2,1:T(8,128)S(1)}, f32[128,16,128]{0,2,1:T(8,128)S(1)}, u32[]{:S(2)}, u32[]{:S(2)}) collective-permute-start(f32[128,16,128]{0,2,1:T(8,128)S(1)} %get-tuple-element.130), channel_id=1, source_target_pairs={{4,0},{8,4},{12,8},{16,12},{20,16},{24,20},{28,24},{32,28},{36,32}... | collective-permute-start | bytes 3145736 | tf_op jit(solution)/shard_map/ppermute | solution.py:14
  114.2 2.3 copy-start
  116.5 30.0 %copy-start.1 = (f32[128,16,128]{2,1,0:T(8,128)}, f32[128,16,128]{2,1,0:T(8,128)S(1)}, u32[]{:S(2)}) copy-start(f32[128,16,128]{2,1,0:T(8,128)S(1)} %fusion.10) | copy-start | bytes 3145732
  116.5 29.7 %copy-start.5 = (bf16[128,2048]{0,1:T(8,128)(2,1)S(1)}, bf16[128,2048]{0,1:T(8,128)(2,1)}, u32[]{:S(2)}) copy-start(bf16[128,2048]{0,1:T(8,128)(2,1)} %copy.65) | copy-start | bytes 1572868
  116.5 29.6 %copy-start.20 = (f32[2048]{0:T(1024)S(1)}, f32[2048]{0:T(1024)}, u32[]{:S(2)}) copy-start(f32[2048]{0:T(1024)} %param.15) | copy-start | bytes 24580
  146.2 1.0 copy-start.2
  159.2 88.9 %collective-permute-start.2 = (bf16[128,2048]{0,1:T(8,128)(2,1)}, bf16[128,2048]{0,1:T(8,128)(2,1)}, u32[]{:S(2)}, u32[]{:S(2)}) collective-permute-start(bf16[128,2048]{0,1:T(8,128)(2,1)} %get-tuple-element.134), channel_id=1, source_target_pairs={{0,4},{4,8},{8,12},{12,16},{16,20},{20,24},{24,28},{28,32},{32,36}... | collective-permute-start | bytes 1572872 | tf_op jit(solution)/shard_map/ppermute | solution.py:14
  163.0 85.1 %collective-permute-start.1 = (bf16[128,2048]{0,1:T(8,128)(2,1)}, bf16[128,2048]{0,1:T(8,128)(2,1)}, u32[]{:S(2)}, u32[]{:S(2)}) collective-permute-start(bf16[128,2048]{0,1:T(8,128)(2,1)} %get-tuple-element.134), channel_id=1, source_target_pairs={{0,8},{4,12},{8,16},{12,20},{16,24},{20,28},{24,32},{28,36},{32,40... | collective-permute-start | bytes 1572872 | tf_op jit(solution)/shard_map/ppermute | solution.py:14
  168.2 71.7 %collective-permute-start.9 = (bf16[127,2048]{0,1:T(8,128)(2,1)}, bf16[127,2048]{0,1:T(8,128)(2,1)}, u32[]{:S(2)}, u32[]{:S(2)}) collective-permute-start(bf16[127,2048]{0,1:T(8,128)(2,1)} %bitcast.150), channel_id=1, source_target_pairs={{4,0},{8,4},{12,8},{16,12},{20,16},{24,20},{28,24},{32,28},{36,32}... | collective-permute-start | bytes 1560584 | tf_op jit(solution)/shard_map/ppermute | solution.py:14
  248.1 2.8 copy-start.13
  249.7 1.2 copy-start.3
  259.8 6.8 %copy-start.9 = (bf16[128,2048]{0,1:T(8,128)(2,1)S(1)}, bf16[128,2048]{0,1:T(8,128)(2,1)}, u32[]{:S(2)}) copy-start(bf16[128,2048]{0,1:T(8,128)(2,1)} %copy-done.8) | copy-start | bytes 1572868
  259.8 6.8 %copy-start.11 = (bf16[128,2048]{0,1:T(8,128)(2,1)S(1)}, bf16[128,2048]{0,1:T(8,128)(2,1)}, u32[]{:S(2)}) copy-start(bf16[128,2048]{0,1:T(8,128)(2,1)} %copy-done.10) | copy-start | bytes 1572868
  259.8 6.8 %copy-start.14 = (f32[128,16,128]{2,1,0:T(8,128)S(1)}, f32[128,16,128]{2,1,0:T(8,128)}, u32[]{:S(2)}) copy-start(f32[128,16,128]{2,1,0:T(8,128)} %fusion.8) | copy-start | bytes 3145732
  263.2 27.1 %collective-permute-start.6 = (f32[128,16,128]{0,2,1:T(8,128)}, f32[128,16,128]{0,2,1:T(8,128)}, u32[]{:S(2)}, u32[]{:S(2)}) collective-permute-start(f32[128,16,128]{0,2,1:T(8,128)} %get-tuple-element.129), channel_id=1, source_target_pairs={{8,0},{12,4},{16,8},{20,12},{24,16},{28,20},{32,24},{36,28},{40,32... | collective-permute-start | bytes 3145736 | tf_op jit(solution)/shard_map/ppermute | solution.py:14
  264.5 37.4 %collective-permute-start.5 = (f32[128,16,128]{0,2,1:T(8,128)}, f32[128,16,128]{0,2,1:T(8,128)}, u32[]{:S(2)}, u32[]{:S(2)}) collective-permute-start(f32[128,16,128]{0,2,1:T(8,128)} %get-tuple-element.128), channel_id=1, source_target_pairs={{4,0},{8,4},{12,8},{16,12},{20,16},{24,20},{28,24},{32,28},{36,32}... | collective-permute-start | bytes 3145736 | tf_op jit(solution)/shard_map/ppermute | solution.py:14
Sparse Core Ops, SparseCore 0:
  240.0 169.8 all-reduce.5
where the time goes:
time: 421 us; the launch traced here: 418 us
  local copies, waits for them, and re-layouts  155 us (37%)
  waiting for transfers between devices  151 us (36%)
  matrix products  35.9 us (9%)
  starting transfers between devices  30.6 us (7%)
  other arithmetic  21.9 us (5%)
  between operations  14.5 us (3%)
  blocking collectives  8.7 us (2%)
    psum x1, waiting for transfers between devices, body(): grad_filters = lax.psum(local_filters, ('context', 'mirror'))  105 us
    ppermute x10, waiting for transfers between devices, passed_along(): return lax.ppermute(block, axis, route)  46.1 us
    another operation x4, local copies, waits for them, and re-layouts, banded(): jnp.tile(band_table, (1, row_count + 1))[:, :row_count * col_count]  35.4 us
    reshape x4, local copies, waits for them, and re-layouts, filter_block(): flattened.reshape(block_size, tok_rows, pad_rows + 1)[:, :, :tap_count]  31.8 us
    ppermute x10, starting transfers between devices, passed_along(): return lax.ppermute(block, axis, route)  30.6 us
    reshape x2, local copies, waits for them, and re-layouts, banded(): return repeated.reshape(band_table.shape[0], row_count, col_count)  25 us
    unnamed x61, local copies, waits for them, and re-layouts  20.7 us
    slice x2, local copies, waits for them, and re-layouts, banded(): jnp.tile(band_table, (1, row_count + 1))[:, :row_count * col_count]  14.1 us
  transfers between devices with their start and end apart: 11, of which 5 were waited for; matrix products, arithmetic and copies ran while one was open for 49% of the time, Pallas kernels for 0%

commit v1 on v0

--- a/solution.py
+++ b/solution.py
@@ -166,7 +166,9 @@
         1, 0, 2, 3
     )
     local_filters = lax.map(filter_block, (grad_blocks, wide_blocks)).reshape(groups, tap_count)
-    grad_filters = lax.psum(local_filters, ("context", "mirror"))
+    grad_filters = local_filters
+    for over in ("context", "mirror"):
+        grad_filters = lax.psum(grad_filters, over)
     return (
         attn_out,
         grad_attn_q,

time: 421 us -> 406 us (0.964)
  waiting for transfers between devices: 151 us -> 131 us
  starting transfers between devices: 30.6 us -> 35.3 us
    psum x1 -> x2, waiting for transfers between devices: 105 us -> 89.6 us  [body(): grad_filters = lax.psum(grad_filters, over)]
    ppermute x10, waiting for transfers between devices: 46.1 us -> 41.3 us  [passed_along(): return lax.ppermute(block, axis, route)]
    ppermute x10, starting transfers between devices: 30.6 us -> 35.3 us  [passed_along(): return lax.ppermute(block, axis, route)]
    unnamed x61 -> x63, local copies, waits for them, and re-layouts: 20.7 us -> 20.8 us
  transfers between devices with their start and end apart: 11 -> 12, of which waited for: 5 -> 4; matrix products, arithmetic and copies ran while one was open for 49% -> 51% of each run, Pallas kernels for 0% -> 0%
where the time goes in v1:
time: 406 us; the launch traced here: 403 us
  local copies, waits for them, and re-layouts  156 us (38%)
  waiting for transfers between devices  131 us (32%)
  matrix products  35.8 us (9%)
  starting transfers between devices  35.3 us (9%)
  other arithmetic  21.7 us (5%)
  between operations  14.6 us (4%)
  blocking collectives  8.69 us (2%)
    psum x2, waiting for transfers between devices, body(): grad_filters = lax.psum(grad_filters, over)  89.6 us
    ppermute x10, waiting for transfers between devices, passed_along(): return lax.ppermute(block, axis, route)  41.3 us
    another operation x4, local copies, waits for them, and re-layouts, banded(): jnp.tile(band_table, (1, row_count + 1))[:, :row_count * col_count]  35.3 us
    ppermute x10, starting transfers between devices, passed_along(): return lax.ppermute(block, axis, route)  35.3 us
    reshape x4, local copies, waits for them, and re-layouts, filter_block(): flattened.reshape(block_size, tok_rows, pad_rows + 1)[:, :, :tap_count]  31.9 us
    reshape x2, local copies, waits for them, and re-layouts, banded(): return repeated.reshape(band_table.shape[0], row_count, col_count)  25.3 us
    unnamed x63, local copies, waits for them, and re-layouts  20.8 us
    slice x2, local copies, waits for them, and re-layouts, banded(): jnp.tile(band_table, (1, row_count + 1))[:, :row_count * col_count]  14.2 us
  transfers between devices with their start and end apart: 12, of which 4 were waited for; matrix products, arithmetic and copies ran while one was open for 51% of the time, Pallas kernels for 0%

profile of v1, /device:TPU:1, one launch (start us, length us, event | category | flops | bytes accessed | tf_op | source)
XLA Modules:
  0.0 403.1 jit_solution(4384621251170008782)
XLA Ops:
  7.2 1.4 copy.70
  8.6 5.1 %collective-permute-start.4 = (bf16[128,2048]{0,1:T(8,128)(2,1)S(1)}, bf16[128,2048]{0,1:T(8,128)(2,1)}, u32[]{:S(2)}, u32[]{:S(2)}) collective-permute-start(bf16[128,2048]{0,1:T(8,128)(2,1)S(1)} %copy.70), channel_id=1, source_target_pairs={{0,4},{4,8},{8,12},{12,16},{16,20},{20,24},{24,28},{28,32},{32,36}... | collective-permute-start | bytes 1572872 | tf_op jit(solution)/shard_map/ppermute | solution.py:14
  13.7 4.3 %collective-permute-start.3 = (bf16[128,2048]{0,1:T(8,128)(2,1)S(1)}, bf16[128,2048]{0,1:T(8,128)(2,1)}, u32[]{:S(2)}, u32[]{:S(2)}) collective-permute-start(bf16[128,2048]{0,1:T(8,128)(2,1)S(1)} %copy.70), channel_id=1, source_target_pairs={{0,8},{4,12},{8,16},{12,20},{16,24},{20,28},{24,32},{28,36},{32,40... | collective-permute-start | bytes 1572872 | tf_op jit(solution)/shard_map/ppermute | solution.py:14
  19.4 1.5 copy.66
  22.9 1.9 collective-permute-start
  28.4 4.4 %tile.8 = bf16[128,129,257]{0,2,1:T(8,128)(2,1)} broadcast(bf16[128,257]{0,1:T(8,128)(2,1)S(1)} %concatenate.19.clone), dimensions={0,2} | broadcast | bytes 8552960 | tf_op jit(solution)/shard_map/tile | solution.py:25
  32.9 13.2 %tile.9 = bf16[128,33153]{0,1:T(8,128)(2,1)} reshape(bf16[128,129,257]{0,2,1:T(8,128)(2,1)} %tile.8) | data formatting | bytes 16974336 | tf_op jit(solution)/shard_map/tile | solution.py:25
  46.1 7.0 %slice.49 = bf16[128,32768]{0,1:T(8,128)(2,1)} slice(bf16[128,33153]{0,1:T(8,128)(2,1)} %tile.9), slice={[0:128], [0:32768]} | slice | bytes 16777216 | tf_op jit(solution)/shard_map/slice | solution.py:25
  53.1 12.4 %copy.69 = bf16[128,128,256]{2,1,0:T(8,128)(2,1)} copy(bf16[128,128,256]{0,2,1:T(8,128)(2,1)} %bitcast.165) | data formatting | bytes 16777216 | tf_op jit(solution)/shard_map/reshape | solution.py:26
  66.1 1.4 pad_maximum_fusion.1
  70.1 1.6 collective-permute-start.8
  71.7 3.2 collective-permute-start.7
  74.9 1.5 maximum_maximum_fusion
  76.5 2.3 fusion.10
  78.8 16.9 %collective-permute-done.8 = f32[128,16,128]{0,2,1:T(8,128)S(1)} collective-permute-done((f32[128,16,128]{0,2,1:T(8,128)S(1)}, f32[128,16,128]{0,2,1:T(8,128)S(1)}, u32[]{:S(2)}, u32[]{:S(2)}) %collective-permute-start.8) | collective-permute-done | bytes 1048608 | tf_op jit(solution)/shard_map/ppermute | solution.py:14
  95.7 12.7 %collective-permute-done.7 = f32[128,16,128]{0,2,1:T(8,128)S(1)} collective-permute-done((f32[128,16,128]{0,2,1:T(8,128)S(1)}, f32[128,16,128]{0,2,1:T(8,128)S(1)}, u32[]{:S(2)}, u32[]{:S(2)}) %collective-permute-start.7) | collective-permute-done | bytes 1048608 | tf_op jit(solution)/shard_map/ppermute | solution.py:14
  109.6 8.7 %all-reduce.3 = (f32[128]{0:T(128)S(1)}, f32[128]{0:T(128)S(1)}) all-reduce(f32[128]{0:T(128)S(1)} %get-tuple-element.111, f32[128]{0:T(128)S(1)} %get-tuple-element.110), channel_id=1, replica_groups=mesh['context'=32,'mirror'=2,'tensor'=4] {'tensor'}, use_global_device_ids=true, to_apply=%region_4.5 | all-reduce | flops 256 | bytes 2048 | tf_op jit(solution)/shard_map/psum | solution.py:68
  118.3 3.4 fusion.45
  121.7 2.1 collective-permute-start.9
  123.8 68.1 %while.13 = (s32[]{:T(128)}, f32[4,32,128]{2,1,0:T(8,128)}, bf16[4,128,32,16]{1,3,2,0:T(8,128)(2,1)}, bf16[4,256,32,16]{1,3,2,0:T(8,128)(2,1)}, s32[256]{0:T(256...) while((s32[]{:T(128)}, f32[4,32,128]{2,1,0:T(8,128)}, bf16[4,128,32,16]{1,3,2,0:T(8,128)(2,1)}, ...), condition=%wide.region_14.15_spmd.clone, body=%wide.region_12.14_spmd.clone.sunk | while | flops 35188736 | bytes 32246372 | solution.py:168
  123.9 1.8 convolution_multiply_fusion.2
  125.7 2.4 copy.103
  128.1 2.3 pad.33
  130.5 8.0 %reshape.319 = f32[32,128,257]{2,1,0:T(8,128)} reshape(f32[32,32896]{1,0:T(8,128)} %pad.33) | data formatting | bytes 8421376 | tf_op jit(solution)/shard_map/while/body/eval_jaxpr/reshape | solution.py:159
  138.4 1.7 slice_reduce_fusion.2
  140.9 1.8 convolution_multiply_fusion.2
  142.7 2.4 copy.103
  145.1 2.3 pad.33
  147.5 8.0 %reshape.319 = f32[32,128,257]{2,1,0:T(8,128)} reshape(f32[32,32896]{1,0:T(8,128)} %pad.33) | data formatting | bytes 8421376 | tf_op jit(solution)/shard_map/while/body/eval_jaxpr/reshape | solution.py:159
  155.5 1.7 slice_reduce_fusion.2
  157.9 1.8 convolution_multiply_fusion.2
  159.7 2.4 copy.103
  162.2 2.3 pad.33
  164.5 8.0 %reshape.319 = f32[32,128,257]{2,1,0:T(8,128)} reshape(f32[32,32896]{1,0:T(8,128)} %pad.33) | data formatting | bytes 8421376 | tf_op jit(solution)/shard_map/while/body/eval_jaxpr/reshape | solution.py:159
  172.5 1.7 slice_reduce_fusion.2
  175.0 1.8 convolution_multiply_fusion.2
  176.8 2.4 copy.103
  179.2 2.3 pad.33
  181.5 8.0 %reshape.319 = f32[32,128,257]{2,1,0:T(8,128)} reshape(f32[32,32896]{1,0:T(8,128)} %pad.33) | data formatting | bytes 8421376 | tf_op jit(solution)/shard_map/while/body/eval_jaxpr/reshape | solution.py:159
  189.5 1.7 slice_reduce_fusion.2
  192.1 4.4 %tile.20 = bf16[128,129,257]{0,2,1:T(8,128)(2,1)} broadcast(bf16[128,257]{0,1:T(8,128)(2,1)S(1)} %concatenate.23.clone), dimensions={0,2} | broadcast | bytes 8552960 | tf_op jit(solution)/shard_map/tile | solution.py:25
  196.6 13.2 %tile.21 = bf16[128,33153]{0,1:T(8,128)(2,1)} reshape(bf16[128,129,257]{0,2,1:T(8,128)(2,1)} %tile.20) | data formatting | bytes 16974336 | tf_op jit(solution)/shard_map/tile | solution.py:25
  209.8 7.1 %slice.57 = bf16[128,32768]{0,1:T(8,128)(2,1)} slice(bf16[128,33153]{0,1:T(8,128)(2,1)} %tile.21), slice={[0:128], [0:32768]} | slice | bytes 16777216 | tf_op jit(solution)/shard_map/slice | solution.py:25
  216.9 12.9 %copy.84 = bf16[128,128,256]{2,1,0:T(8,128)(2,1)} copy(bf16[128,128,256]{0,2,1:T(8,128)(2,1)} %bitcast.166) | data formatting | bytes 16777216 | tf_op jit(solution)/shard_map/reshape | solution.py:26
  229.7 3.7 collective-permute-start.2
  233.5 5.2 %collective-permute-start.1 = (bf16[128,2048]{0,1:T(8,128)(2,1)}, bf16[128,2048]{0,1:T(8,128)(2,1)}, u32[]{:S(2)}, u32[]{:S(2)}) collective-permute-start(bf16[128,2048]{0,1:T(8,128)(2,1)} %get-tuple-element.134), channel_id=1, source_target_pairs={{0,8},{4,12},{8,16},{12,20},{16,24},{20,28},{24,32},{28,36},{32,40... | collective-permute-start | bytes 1572872 | tf_op jit(solution)/shard_map/ppermute | solution.py:14
  238.7 2.0 copy.88
  240.7 89.6 %all-reduce.7.cloned.1.call-done = f32[128,128]{1,0:T(8,128)} async-done(((f32[128,128]{1,0:T(8,128)}), f32[128,128]{1,0:T(8,128)}) %all-reduce.7.cloned.1.call-update) | async-done | bytes 65552 | tf_op jit(solution)/shard_map/psum | solution.py:171
  330.4 1.4 maximum_maximum_fusion.1
  331.8 6.7 %fusion.8 = f32[128,16,128]{2,1,0:T(8,128)} fusion(bf16[256,128,16]{0,2,1:T(8,128)(2,1)S(1)} %bitcast.175, bf16[128,128,256]{2,1,0:T(8,128)(2,1)} %copy.84, bf16[128,256]{1,0:T(8,128)(2,1)S(1)} %get-tuple-element.137), kind=kOutput, calls=%fused_computation.11 | convolution fusion | flops 138412032 | bytes 10551296 | tf_op jit(solution)/shard_map/gtu,ugc->tgc/dot_general | solution.py:138
  338.6 1.5 pad_maximum_fusion
  341.2 2.4 fusion.72
  343.6 6.6 %convolution_bitcast_fusion.1 = f32[384,16,128]{0,2,1:T(8,128)} fusion(bf16[128,16,128]{0,2,1:T(8,128)(2,1)} %bitcast.177, f32[16,384,128]{2,1,0:T(8,128)} %fusion.72, f32[16,384,128]{2,1,0:T(8,128)S(1)} %get-tuple-element.142, f32[16,128]{1,0:T(8,128)S(1)} %log_add_fusion, pred[128,384]{0,1:T(8,128)(4,1)S(1)} %fusion.54), kind=kOutput, calls=%fused_computation.32 | convolution fusion | flops 209979776 | bytes 10018816 | tf_op jit(solution)/shard_map/htu,thd->uhd/dot_general | solution.py:107
  350.2 3.3 fusion.70
  354.7 6.9 %collective-permute-start.5 = (f32[128,16,128]{0,2,1:T(8,128)}, f32[128,16,128]{0,2,1:T(8,128)}, u32[]{:S(2)}, u32[]{:S(2)}) collective-permute-start(f32[128,16,128]{0,2,1:T(8,128)} %get-tuple-element.128), channel_id=1, source_target_pairs={{4,0},{8,4},{12,8},{16,12},{20,16},{24,20},{28,24},{32,28},{36,32}... | collective-permute-start | bytes 3145736 | tf_op jit(solution)/shard_map/ppermute | solution.py:14
  362.8 2.0 copy.89
  364.9 2.0 copy.90
  366.9 3.0 convolution_convert_fusion
  369.8 2.0 copy.85
  371.9 6.1 %fusion.44 = bf16[16,128,128]{2,1,0:T(8,128)(2,1)} fusion(bf16[384,16,128]{0,2,1:T(8,128)(2,1)} %bitcast.172, f32[16,384,128]{2,1,0:T(8,128)} %fusion.72, f32[16,384,128]{2,1,0:T(8,128)S(1)} %get-tuple-element.142, f32[16,128]{1,0:T(8,128)S(1)} %log_add_fusion, pred[128,384]{0,1:T(8,128)(4,1)S(1)} %fusion.54), kind=kOutput, calls=%fused_computation.54 | convolution fusion | flops 210241920 | bytes 8445952 | tf_op jit(solution)/shard_map/htu,uhd->thd/dot_general | solution.py:102
  378.0 2.0 copy.86
  380.1 11.7 %collective-permute-done.5 = f32[128,16,128]{0,2,1:T(8,128)} collective-permute-done((f32[128,16,128]{0,2,1:T(8,128)}, f32[128,16,128]{0,2,1:T(8,128)}, u32[]{:S(2)}, u32[]{:S(2)}) %collective-permute-start.5) | collective-permute-done | bytes 1048608 | tf_op jit(solution)/shard_map/ppermute | solution.py:14
  391.8 2.0 fusion.51
  394.8 1.5 copy.115
  (109 shorter events, 19.1 us)
Async XLA Ops:
  7.2 17.6 %copy-start.17 = (bf16[128,2048]{1,0:T(8,128)(2,1)S(1)}, bf16[128,2048]{1,0:T(8,128)(2,1)}, u32[]{:S(2)}) copy-start(bf16[128,2048]{1,0:T(8,128)(2,1)} %param.11) | copy-start | bytes 1572868
  7.2 323.1 %all-reduce.7.cloned.1.call-start = ((), (), s32[]{:S(2)}) async-start(), calls=%async_computation | async-start | bytes 131072 | tf_op jit(solution)/shard_map/psum | solution.py:171
  8.6 17.2 %copy-start.18 = (bf16[128,2048]{1,0:T(8,128)(2,1)S(1)}, bf16[128,2048]{1,0:T(8,128)(2,1)}, u32[]{:S(2)}) copy-start(bf16[128,2048]{1,0:T(8,128)(2,1)} %param.18) | copy-start | bytes 1572868
  8.6 57.4 %collective-permute-start.4 = (bf16[128,2048]{0,1:T(8,128)(2,1)S(1)}, bf16[128,2048]{0,1:T(8,128)(2,1)}, u32[]{:S(2)}, u32[]{:S(2)}) collective-permute-start(bf16[128,2048]{0,1:T(8,128)(2,1)S(1)} %copy.70), channel_id=1, source_target_pairs={{0,4},{4,8},{8,12},{12,16},{16,20},{20,24},{24,28},{28,32},{32,36}... | collective-permute-start | bytes 1572872 | tf_op jit(solution)/shard_map/ppermute | solution.py:14
  13.7 52.4 %collective-permute-start.3 = (bf16[128,2048]{0,1:T(8,128)(2,1)S(1)}, bf16[128,2048]{0,1:T(8,128)(2,1)}, u32[]{:S(2)}, u32[]{:S(2)}) collective-permute-start(bf16[128,2048]{0,1:T(8,128)(2,1)S(1)} %copy.70), channel_id=1, source_target_pairs={{0,8},{4,12},{8,16},{12,20},{16,24},{20,28},{24,32},{28,36},{32,40... | collective-permute-start | bytes 1572872 | tf_op jit(solution)/shard_map/ppermute | solution.py:14
  19.3 8.8 %copy-start.8 = (bf16[128,2048]{0,1:T(8,128)(2,1)}, bf16[128,2048]{0,1:T(8,128)(2,1)S(1)}, u32[]{:S(2)}) copy-start(bf16[128,2048]{0,1:T(8,128)(2,1)S(1)} %copy.67) | copy-start | bytes 1572868
  19.3 7.5 %copy-start.22 = (s32[4]{0:T(128)S(1)}, s32[4]{0:T(128)}, u32[]{:S(2)}) copy-start(s32[4]{0:T(128)} %param.19) | copy-start | bytes 52
  19.4 7.8 %copy-start.19 = (bf16[128,2048]{1,0:T(8,128)(2,1)S(1)}, bf16[128,2048]{1,0:T(8,128)(2,1)}, u32[]{:S(2)}) copy-start(bf16[128,2048]{1,0:T(8,128)(2,1)} %param.16) | copy-start | bytes 1572868
  20.9 12.0 %copy-start.10 = (bf16[128,2048]{0,1:T(8,128)(2,1)}, bf16[128,2048]{0,1:T(8,128)(2,1)S(1)}, u32[]{:S(2)}) copy-start(bf16[128,2048]{0,1:T(8,128)(2,1)S(1)} %copy.66) | copy-start | bytes 1572868
  20.9 7.3 %copy-start.20 = (bf16[128,128]{1,0:T(8,128)(2,1)S(1)}, bf16[128,128]{1,0:T(8,128)(2,1)}, u32[]{:S(2)}) copy-start(bf16[128,128]{1,0:T(8,128)(2,1)} %param.14) | copy-start | bytes 98308
  21.1 0.8 copy-start.6
  22.9 52.0 %collective-permute-start = (bf16[127,2048]{0,1:T(8,128)(2,1)}, bf16[127,2048]{0,1:T(8,128)(2,1)}, u32[]{:S(2)}, u32[]{:S(2)}) collective-permute-start(bf16[127,2048]{0,1:T(8,128)(2,1)} %slice.48), channel_id=1, source_target_pairs={{0,4},{4,8},{8,12},{12,16},{16,20},{20,24},{24,28},{28,32},{32,36}... | collective-permute-start | bytes 1560584 | tf_op jit(solution)/shard_map/ppermute | solution.py:14
  65.5 1.9 copy-start.16
  67.5 1.5 copy-start.4
  67.5 1.5 copy-start.12
  68.3 8.1 %slice-start = ((s8[8388608]{0:T(1024)(128)(4,1)}), s8[4194304]{0:T(1024)(128)(4,1)S(1)}, s32[]{:S(2)}) async-start(s8[8388608]{0:T(1024)(128)(4,1)} %bitcast.163), calls=%async_computation.2 | async-start | bytes 8388608
  69.0 7.4 %slice-start.1 = ((s8[8388608]{0:T(1024)(128)(4,1)}), s8[4194304]{0:T(1024)(128)(4,1)S(1)}, s32[]{:S(2)}) async-start(s8[8388608]{0:T(1024)(128)(4,1)} %bitcast.163), calls=%async_computation.3 | async-start | bytes 8388608
  69.8 5.0 %copy-start.7 = (bf16[128,2048]{0,1:T(8,128)(2,1)S(1)}, bf16[128,2048]{0,1:T(8,128)(2,1)}, u32[]{:S(2)}) copy-start(bf16[128,2048]{0,1:T(8,128)(2,1)} %copy-done.6) | copy-start | bytes 1572868
  70.1 25.6 %collective-permute-start.8 = (f32[128,16,128]{0,2,1:T(8,128)S(1)}, f32[128,16,128]{0,2,1:T(8,128)S(1)}, u32[]{:S(2)}, u32[]{:S(2)}) collective-permute-start(f32[128,16,128]{0,2,1:T(8,128)S(1)} %get-tuple-element.131), channel_id=1, source_target_pairs={{8,0},{12,4},{16,8},{20,12},{24,16},{28,20},{32,24},{36,28},{40,32... | collective-permute-start | bytes 3145736 | tf_op jit(solution)/shard_map/ppermute | solution.py:14
  71.7 36.7 %collective-permute-start.7 = (f32[128,16,128]{0,2,1:T(8,128)S(1)}, f32[128,16,128]{0,2,1:T(8,128)S(1)}, u32[]{:S(2)}, u32[]{:S(2)}) collective-permute-start(f32[128,16,128]{0,2,1:T(8,128)S(1)} %get-tuple-element.130), channel_id=1, source_target_pairs={{4,0},{8,4},{12,8},{16,12},{20,16},{24,20},{28,24},{32,28},{36,32}... | collective-permute-start | bytes 3145736 | tf_op jit(solution)/shard_map/ppermute | solution.py:14
  76.4 2.3 copy-start
  78.7 30.2 %copy-start.1 = (f32[128,16,128]{2,1,0:T(8,128)}, f32[128,16,128]{2,1,0:T(8,128)S(1)}, u32[]{:S(2)}) copy-start(f32[128,16,128]{2,1,0:T(8,128)S(1)} %fusion.10) | copy-start | bytes 3145732
  78.7 29.8 %copy-start.5 = (bf16[128,2048]{0,1:T(8,128)(2,1)S(1)}, bf16[128,2048]{0,1:T(8,128)(2,1)}, u32[]{:S(2)}) copy-start(bf16[128,2048]{0,1:T(8,128)(2,1)} %copy.65) | copy-start | bytes 1572868
  78.8 29.8 %copy-start.21 = (f32[2048]{0:T(1024)S(1)}, f32[2048]{0:T(1024)}, u32[]{:S(2)}) copy-start(f32[2048]{0:T(1024)} %param.15) | copy-start | bytes 24580
  108.6 1.0 copy-start.2
  121.7 208.7 %collective-permute-start.9 = (bf16[127,2048]{0,1:T(8,128)(2,1)}, bf16[127,2048]{0,1:T(8,128)(2,1)}, u32[]{:S(2)}, u32[]{:S(2)}) collective-permute-start(bf16[127,2048]{0,1:T(8,128)(2,1)} %bitcast.150), channel_id=1, source_target_pairs={{4,0},{8,4},{12,8},{16,12},{20,16},{24,20},{28,24},{32,28},{36,32}... | collective-permute-start | bytes 1560584 | tf_op jit(solution)/shard_map/ppermute | solution.py:14
  191.9 202.9 %all-reduce.9.cloned.1.call-start = ((), (), s32[]{:S(2)}) async-start(), calls=%async_computation.1 | async-start | bytes 131072 | tf_op jit(solution)/shard_map/psum | solution.py:171
  229.7 108.8 %collective-permute-start.2 = (bf16[128,2048]{0,1:T(8,128)(2,1)}, bf16[128,2048]{0,1:T(8,128)(2,1)}, u32[]{:S(2)}, u32[]{:S(2)}) collective-permute-start(bf16[128,2048]{0,1:T(8,128)(2,1)} %get-tuple-element.134), channel_id=1, source_target_pairs={{0,4},{4,8},{8,12},{12,16},{16,20},{20,24},{24,28},{28,32},{32,36}... | collective-permute-start | bytes 1572872 | tf_op jit(solution)/shard_map/ppermute | solution.py:14
  233.5 105.1 %collective-permute-start.1 = (bf16[128,2048]{0,1:T(8,128)(2,1)}, bf16[128,2048]{0,1:T(8,128)(2,1)}, u32[]{:S(2)}, u32[]{:S(2)}) collective-permute-start(bf16[128,2048]{0,1:T(8,128)(2,1)} %get-tuple-element.134), channel_id=1, source_target_pairs={{0,8},{4,12},{8,16},{12,20},{16,24},{20,28},{24,32},{28,36},{32,40... | collective-permute-start | bytes 1572872 | tf_op jit(solution)/shard_map/ppermute | solution.py:14
  331.8 6.7 %copy-start.15 = (bf16[128,2048]{0,1:T(8,128)(2,1)S(1)}, bf16[128,2048]{0,1:T(8,128)(2,1)}, u32[]{:S(2)}) copy-start(bf16[128,2048]{0,1:T(8,128)(2,1)} %get-tuple-element.134) | copy-start | bytes 1572868
  338.5 2.7 copy-start.13
  340.0 1.2 copy-start.3
  350.2 11.4 %copy-start.9 = (bf16[128,2048]{0,1:T(8,128)(2,1)S(1)}, bf16[128,2048]{0,1:T(8,128)(2,1)}, u32[]{:S(2)}) copy-start(bf16[128,2048]{0,1:T(8,128)(2,1)} %copy-done.8) | copy-start | bytes 1572868
  350.2 11.4 %copy-start.11 = (bf16[128,2048]{0,1:T(8,128)(2,1)S(1)}, bf16[128,2048]{0,1:T(8,128)(2,1)}, u32[]{:S(2)}) copy-start(bf16[128,2048]{0,1:T(8,128)(2,1)} %copy-done.10) | copy-start | bytes 1572868
  350.2 11.4 %copy-start.14 = (f32[128,16,128]{2,1,0:T(8,128)S(1)}, f32[128,16,128]{2,1,0:T(8,128)}, u32[]{:S(2)}) copy-start(f32[128,16,128]{2,1,0:T(8,128)} %fusion.8) | copy-start | bytes 3145732
  353.4 26.6 %collective-permute-start.6 = (f32[128,16,128]{0,2,1:T(8,128)}, f32[128,16,128]{0,2,1:T(8,128)}, u32[]{:S(2)}, u32[]{:S(2)}) collective-permute-start(f32[128,16,128]{0,2,1:T(8,128)} %get-tuple-element.129), channel_id=1, source_target_pairs={{8,0},{12,4},{16,8},{20,12},{24,16},{28,20},{32,24},{36,28},{40,32... | collective-permute-start | bytes 3145736 | tf_op jit(solution)/shard_map/ppermute | solution.py:14
  354.7 37.0 %collective-permute-start.5 = (f32[128,16,128]{0,2,1:T(8,128)}, f32[128,16,128]{0,2,1:T(8,128)}, u32[]{:S(2)}, u32[]{:S(2)}) collective-permute-start(f32[128,16,128]{0,2,1:T(8,128)} %get-tuple-element.128), channel_id=1, source_target_pairs={{4,0},{8,4},{12,8},{16,12},{20,16},{24,20},{28,24},{32,28},{36,32}... | collective-permute-start | bytes 3145736 | tf_op jit(solution)/shard_map/ppermute | solution.py:14
Sparse Core Ops, SparseCore 0:
  192.1 138.2 all-reduce.6
  332.9 31.7 all-reduce.8
